TPU v7x, 32 devices: a whole 2x2x4 slice. The times are simulated.
32 devices in a mesh: groups: 2 (over x), mix: 16 (over z, y, core).
Axes of the slice: x: 2, y: 2, z: 4, core: 2. Of those that a mesh axis runs over, the one named last changes fastest.
Arguments:
- resid_in: bfloat16 [4096, 2048], P(('groups', 'mix')), parts along dimension 0, may hold values from -40 to 40
- head_in: bfloat16 [4096, 4096], P('groups', 'mix'), parts along dimension 0, may hold values from -6 to 6
- gate_in: bfloat16 [4096, 4096], P('groups', 'mix'), parts along dimension 0, may hold values from -64 to 64
- in_basis: bfloat16 [4096, 128], P('groups'), parts along dimension 0, may hold values from -6 to 6
- out_basis: bfloat16 [4096, 128], P('groups'), parts along dimension 0, may hold values from -6 to 6
- step_size: float32 [64, 4096], P('mix', 'groups'), parts along dimension 1, may hold values from 0 to 2
- decay_rate: float32 [64], P('mix'), may hold values from 0.5 to 2
- init_state: float32 [16, 64, 64, 128], P('groups', 'mix'), parts along dimension 0, may hold values from -0.6 to 0.6
- lengths: int32 [16], P('groups'), parts along dimension 0, may hold values from 1 to 512, 2048 in all
- norm_gain: float32 [4096], replicated, may hold values from 0.1 to 1.9
- out_proj: bfloat16 [4096, 2048], P('mix'), may hold values from -0.09375 to 0.09375
- moe_gain: float32 [2048], replicated, may hold values from 0.1 to 1.9
- expert_ids: int32 [4096, 8], P(('groups', 'mix')), parts along dimension 0, may hold values from 0 to 31, as said below
- route_weight: float32 [4096, 8], P(('groups', 'mix')), parts along dimension 0, may hold values from 0.1 to 0.4
- placement: int32 [32], replicated, may hold values from 0 to 31, each once
- w_gate: bfloat16 [32, 2048, 768], P('mix'), may hold values from -0.125 to 0.125
- w_up: bfloat16 [32, 2048, 768], P('mix'), may hold values from -0.125 to 0.125
- w_down: bfloat16 [32, 768, 2048], P('mix'), may hold values from -0.21875 to 0.21875
Outputs:
- layer_out: bfloat16 [4096, 2048], P(('groups', 'mix')), parts along dimension 0
There are 2 independent parts, one for each index of `groups`. A program takes and returns all parts, laid end to end along the dimension named above; an argument that names none is the same for every part. Nothing has to cross between parts.
Inputs may be any that keep to these rules, and one draw needn't show every extreme that they name: `expert_ids`: each row names 8 different experts. Within each aligned block of 128 rows (one device's rows), 8 experts appear exactly 64 times each, 8 others 64 / 2 times each and the rest 64 / 4 times each; each of the three sets is the same in every block. `placement`: each slot once. `lengths`: requests fill the 2048 positions in order.
All inputs are finite; a program needn't handle non-finite values.
Results may differ from a plain program's by a relative error of at most 0.013.
Values may be sent and summed in bfloat16 or wider, within the bound.
No kernel may reach another device: no remote copies, remote signals or barrier semaphores. Data moves between devices by JAX's collectives and lax.ppermute only.
A program may use at most 128 MiB of HBM per device.

v0:
```python
import jax
import jax.numpy as jnp
from jax import lax
from jax.sharding import PartitionSpec as P

HEADS = 64
HEAD_DIM = 64
SPAN = 256
epsilon = 1e-05


def request_layout(lengths, tokens_total):
    request_end = jnp.cumsum(lengths)
    request_first = request_end - lengths
    position = jnp.arange(tokens_total, dtype=jnp.int32)
    segment = jnp.sum((position[None, :] >= request_end[:, None]).astype(jnp.int32), axis=0)
    member = segment[None, :] == jnp.arange(lengths.shape[0], dtype=jnp.int32)[:, None]
    first_of = jnp.sum(jnp.where(member, request_first[:, None], 0), axis=0)
    return (segment, first_of, member)


def scan_heads(
    head_values,
    head_steps,
    head_rates,
    in_basis,
    out_basis,
    state_init,
    segment,
    first_of,
    member,
    block_len,
):
    tokens_total = head_values.shape[0]
    local_heads = head_steps.shape[0]
    head_width = head_values.shape[1] // local_heads
    blocks = tokens_total // block_len
    highest = lax.Precision.HIGHEST
    log_decay = -head_steps * head_rates[:, None]
    driven = (
        head_values.reshape(tokens_total, local_heads, head_width)
        .transpose(1, 0, 2)
        .astype(jnp.float32)
    )
    driven = driven * head_steps[:, :, None]
    drive_split = driven.reshape(local_heads, blocks, block_len, head_width).transpose(1, 0, 2, 3)
    decay_split = log_decay.reshape(local_heads, blocks, block_len).transpose(1, 0, 2)

    def split_rows(array):
        return array.reshape((blocks, block_len) + array.shape[1:])

    block_first = jnp.arange(blocks, dtype=jnp.int32) * block_len
    member_blocks = member.reshape(member.shape[0], blocks, block_len).transpose(1, 0, 2)
    init_heads = state_init.transpose(1, 0, 2, 3)
    inputs = (
        drive_split,
        decay_split,
        split_rows(in_basis),
        split_rows(out_basis),
        split_rows(segment),
        split_rows(first_of),
        member_blocks,
        block_first,
    )
    offsets = jnp.arange(block_len, dtype=jnp.int32)
    causal = offsets[None, :] <= offsets[:, None]

    def advance(states_in, block_in):
        (
            drive_heads,
            decay_heads,
            basis_block,
            readout_block,
            segment_block,
            first_block,
            member_block,
            first_pos,
        ) = block_in
        basis_wide = basis_block.astype(jnp.float32)
        readout_wide = readout_block.astype(jnp.float32)
        same_seq = (segment_block[:, None] == segment_block[None, :]) & causal
        scores = jnp.dot(readout_block, basis_block.T, preferred_element_type=jnp.float32)
        carried = first_block < first_pos
        member_wide = member_block.astype(jnp.float32)

        def one_head(state_in, drive_block, decay_block, head_init):
            running = jnp.cumsum(decay_block)
            earlier = running - decay_block
            gap_values = jnp.minimum(running[:, None] - running[None, :], 0.0)
            kernel = jnp.where(same_seq, jnp.exp(gap_values), 0.0)
            output = jnp.dot(kernel * scores, drive_block, precision=highest)
            before = jnp.max(jnp.where(same_seq, earlier[None, :], -jnp.inf), axis=1)
            weight = jnp.exp(running - before)
            from_state = jnp.dot(readout_wide, state_in.T, precision=highest)
            projected = jnp.einsum("qn,rpn->rqp", readout_wide, head_init, precision=highest)
            from_init = jnp.sum(member_wide[:, :, None] * projected, axis=0)
            output = output + weight[:, None] * jnp.where(carried[:, None], from_state, from_init)
            last_weight = jnp.where(same_seq[-1], jnp.exp(running[-1] - running), 0.0)
            state_out = jnp.dot(
                (drive_block * last_weight[:, None]).T, basis_wide, precision=highest
            )
            init_last = jnp.einsum("r,rpn->pn", member_wide[:, -1], head_init, precision=highest)
            source = jnp.where(carried[-1], state_in, init_last)
            state_out = state_out + weight[-1] * source
            return (state_out, output)

        return jax.vmap(one_head)(states_in, drive_heads, decay_heads, init_heads)

    empty_state = jnp.zeros((local_heads, head_width, in_basis.shape[1]), jnp.float32)
    _, outputs = lax.scan(advance, empty_state, inputs)
    return outputs.transpose(0, 2, 1, 3).reshape(tokens_total, local_heads * head_width)


def local(
    resid_in,
    head_in,
    gate_in,
    in_basis,
    out_basis,
    step_size,
    decay_rate,
    init_state,
    lengths,
    norm_gain,
    out_proj,
    moe_gain,
    expert_ids,
    route_weight,
    placement,
    w_gate,
    w_up,
    w_down,
):
    tokens_total = head_in.shape[0]
    model_width = out_proj.shape[1]
    devices = lax.axis_size("mix")
    tok_rows = tokens_total // devices
    segment, first_of, member = request_layout(lengths, tokens_total)
    scan_out = scan_heads(
        head_in,
        step_size,
        decay_rate,
        in_basis,
        out_basis,
        init_state,
        segment,
        first_of,
        member,
        SPAN,
    )
    gated_out = scan_out * jax.nn.silu(gate_in.astype(jnp.float32))
    regrouped = lax.all_to_all(
        gated_out.astype(jnp.bfloat16), "mix", split_axis=0, concat_axis=1, tiled=True
    ).astype(gated_out.dtype)
    squares = jnp.sum(regrouped * regrouped, axis=1)
    mixed_in = (regrouped * norm_gain).astype(jnp.bfloat16)
    full_proj = lax.all_gather(out_proj, "mix", axis=0, tiled=True)
    group_terms = jnp.einsum(
        "tgc,gcd->tgd",
        mixed_in.reshape(tok_rows, devices, -1),
        full_proj.reshape(devices, -1, model_width),
        preferred_element_type=jnp.float32,
    ).astype(jnp.bfloat16)
    group_terms = lax.optimization_barrier(group_terms)
    mixer_sum = jnp.sum(group_terms.astype(jnp.float32), axis=1)
    mixer_out = mixer_sum * lax.rsqrt(squares / (HEADS * HEAD_DIM) + epsilon)[:, None]
    hidden = resid_in.astype(jnp.float32) + mixer_out
    normed = (
        hidden * lax.rsqrt(jnp.mean(hidden * hidden, axis=1, keepdims=True) + epsilon) * moe_gain
    ).astype(jnp.bfloat16)
    top_count = expert_ids.shape[1]
    flat_ids = expert_ids.reshape(-1)
    pair_count = flat_ids.shape[0]
    experts_total = placement.shape[0]
    cap_slots = 2 * pair_count // experts_total
    choose = (flat_ids[:, None] == jnp.arange(experts_total, dtype=jnp.int32)[None, :]).astype(
        jnp.int32
    )
    slot_of = jnp.sum(choose * placement[None, :], axis=1)
    slot_rank = jnp.sum(jnp.cumsum(choose, axis=0) * choose, axis=1) - 1
    buffer_index = slot_of * cap_slots + slot_rank
    owner_token = (
        jnp.full((experts_total * cap_slots,), -1, jnp.int32)
        .at[buffer_index]
        .set(jnp.arange(pair_count, dtype=jnp.int32) // top_count)
    )
    filled = owner_token >= 0
    send_rows = jnp.where(
        filled[:, None],
        jnp.take(normed, jnp.maximum(owner_token, 0), axis=0),
        jnp.zeros((), jnp.bfloat16),
    )
    send_rows = send_rows.reshape(devices, experts_total // devices, cap_slots, model_width)
    received = lax.all_to_all(send_rows, "mix", split_axis=0, concat_axis=0, tiled=True)
    gate_part = jnp.einsum("sekd,edf->sekf", received, w_gate, preferred_element_type=jnp.float32)
    up_part = jnp.einsum("sekd,edf->sekf", received, w_up, preferred_element_type=jnp.float32)
    inner_act = (jax.nn.silu(gate_part) * up_part).astype(jnp.bfloat16)
    result = jnp.einsum(
        "sekf,efd->sekd", inner_act, w_down, preferred_element_type=jnp.float32
    ).astype(jnp.bfloat16)
    returned_rows = lax.all_to_all(result, "mix", split_axis=0, concat_axis=0, tiled=True)
    back_flat = returned_rows.reshape(experts_total * cap_slots, model_width)
    picked = jnp.take(back_flat, buffer_index, axis=0).reshape(tok_rows, top_count, model_width)
    expert_sum = jnp.sum(route_weight[:, :, None] * picked.astype(jnp.float32), axis=1)
    return (hidden + expert_sum).astype(jnp.bfloat16)


def solution(mesh):
    return jax.shard_map(
        local,
        mesh=mesh,
        in_specs=(
            P(("groups", "mix"), None),
            P("groups", "mix"),
            P("groups", "mix"),
            P("groups", None),
            P("groups", None),
            P("mix", "groups"),
            P("mix"),
            P("groups", "mix", None, None),
            P("groups"),
            P(),
            P("mix", None),
            P(),
            P(("groups", "mix"), None),
            P(("groups", "mix"), None),
            P(),
            P("mix", None, None),
            P("mix", None, None),
            P("mix", None, None),
        ),
        out_specs=P(("groups", "mix"), None),
        check_vma=False,
    )
```

profile of v0, /device:TPU:15, one launch (start us, length us, event | category | flops | bytes accessed | tf_op | source)
XLA Modules:
  0.0 655.7 jit_solution(5398734231998708079)
XLA Ops:
  11.5 2.2 copy.110
  15.5 123.0 %while.13 = (s32[]{:T(128)}, f32[4,64,128]{2,1,0:T(8,128)S(1)}, f32[8,4,256,64]{2,3,1,0:T(8,128)}, f32[8,4,256,64]{2,0,3,1:T(8,128)}, s32[8,256]{1,0:T(8,128)S(1...) while((s32[]{:T(128)}, f32[4,64,128]{2,1,0:T(8,128)S(1)}, ...), condition=%wide.region_8.9_spmd.clone, body=%wide.region_3.8_spmd.clone.sunk | while | flops 1231164672 | bytes 6564249 | solution.py:110
  17.8 1.9 fusion.115
  25.0 2.2 fusion.116
  40.4 2.1 fusion.116
  48.6 1.9 fusion.115
  55.8 2.2 fusion.116
  64.0 1.9 fusion.115
  71.2 2.2 fusion.116
  86.6 2.2 fusion.116
  101.9 2.1 fusion.116
  117.3 2.1 fusion.116
  125.5 1.9 fusion.115
  132.6 2.2 fusion.116
  138.5 2.9 copy.89
  147.0 6.7 %all-to-all-start = ((bf16[16,128,256]{2,1,0:T(8,128)(2,1)}), bf16[16,128,256]{2,1,0:T(8,128)(2,1)S(1)}, u32[]{:S(2)}, u32[]{:S(2)}) async-start(bf16[16,128,256]{2,1,0:T(8,128)(2,1)} %bitcast.11), calls=%async_computation | async-start | bytes 2097152 | tf_op jit(solution)/shard_map/all_to_all | solution.py:152
  154.1 9.0 %reduce-window.26 = s32[32,8,128]{2,1,0:T(8,128)S(1)} reduce-window(s32[32,8,128]{2,1,0:T(8,128)S(1)} %fusion.68, s32[]{:T(128)} %constant.97.clone.1), window={size=1x1x128 pad=0_0x0_0x127_0}, to_apply=%region_12.13 | reduce-window | flops 4161536 | bytes 262148 | tf_op jit(solution)/shard_map/reduce-window.3
  163.7 4.3 scatter_custom_fusion
  168.2 10.4 %all-to-all-done = bf16[16,128,256]{2,1,0:T(8,128)(2,1)S(1)} async-done(((bf16[16,128,256]{2,1,0:T(8,128)(2,1)}), bf16[16,128,256]{2,1,0:T(8,128)(2,1)S(1)}, u32[]{:S(2)}, u32[]{:S(2)}) %all-to-all-start) | async-done | bytes 1048608 | tf_op jit(solution)/shard_map/all_to_all | solution.py:152
  178.9 11.4 %convert_bitcast_fusion.1 = bf16[128,16,2048]{2,0,1:T(8,128)(2,1)} fusion(bf16[16,256,2048]{2,1,0:T(8,128)(2,1)} %bitcast.224, bf16[16,128,256]{2,1,0:T(8,128)(2,1)S(1)} %all-to-all-done, f32[16,256]{1,0:T(8,128)S(1)} %mul.163), kind=kOutput, calls=%fused_computation.66 | convolution fusion | flops 2153250816 | bytes 26230784 | tf_op jit(solution)/shard_map/tgc,gcd->tgd/dot_general | solution.py:158
  190.3 5.3 convert_reduce_fusion
  196.3 11.0 %gather_fusion = bf16[2048,2048]{1,0:T(8,128)(2,1)} fusion(bf16[128,2048]{1,0:T(8,128)(2,1)S(1)} %multiply_convert_fusion, s32[2048]{0:T(1024)S(1)} %maximum_clamp_fusion), kind=kCustom, calls=%fused_computation | custom fusion | bytes 16785408 | tf_op jit(solution)/shard_map/jit(_take)/gather | solution.py:190
  207.3 4.6 select_select_fusion
  212.0 187.0 %all_to_all.23 = bf16[16,2,64,2048]{3,2,1,0:T(8,128)(2,1)S(1)} all-to-all(bf16[16,2,64,2048]{3,2,1,0:T(8,128)(2,1)S(1)} %select_select_fusion), channel_id=1, replica_groups=mesh['groups'=2,'mix'=16] {'mix'}, dimensions={0} | all-to-all | bytes 16777216 | tf_op jit(solution)/shard_map/all_to_all | solution.py:194
  398.9 10.6 %fusion.39 = f32[2,16,64,768]{3,2,1,0:T(8,128)} fusion(bf16[16,2,64,2048]{3,2,1,0:T(8,128)(2,1)S(1)} %all_to_all.23, bf16[2,2048,768]{2,1,0:T(8,128)(2,1)} %param.36), kind=kOutput, calls=%fused_computation.67 | convolution fusion | flops 6442450944 | bytes 20971520 | tf_op jit(solution)/shard_map/sekd,edf->sekf/dot_general | solution.py:196
  409.6 8.5 %fusion.41 = f32[2,16,64,768]{3,2,1,0:T(8,128)} fusion(bf16[16,2,64,2048]{3,2,1,0:T(8,128)(2,1)S(1)} %all_to_all.23, bf16[2,2048,768]{2,1,0:T(8,128)(2,1)S(1)} %bitcast.249), kind=kOutput, calls=%fused_computation.69 | convolution fusion | flops 6442450944 | bytes 20971520 | tf_op jit(solution)/shard_map/sekd,edf->sekf/dot_general | solution.py:195
  418.1 14.5 %convert_bitcast_fusion = bf16[16,2,64,2048]{3,2,0,1:T(8,128)(2,1)} fusion(bf16[2,768,2048]{2,1,0:T(8,128)(2,1)} %param.37, f32[2,16,64,768]{3,2,1,0:T(8,128)} %fusion.39, f32[2,16,64,768]{3,2,1,0:T(8,128)} %fusion.41), kind=kOutput, calls=%fused_computation.64 | convolution fusion | flops 6456082432 | bytes 27262976 | tf_op jit(solution)/shard_map/sekf,efd->sekd/dot_general | solution.py:198
  432.6 8.3 %copy.99 = bf16[16,2,64,2048]{3,2,1,0:T(8,128)(2,1)} copy(bf16[16,2,64,2048]{3,2,0,1:T(8,128)(2,1)} %convert_bitcast_fusion) | data formatting | bytes 16777216 | tf_op jit(solution)/shard_map/convert_element_type | solution.py:200
  440.8 5.7 all-to-all-start.2
  446.8 182.1 %all-to-all-done.2 = bf16[16,2,64,2048]{3,2,1,0:T(8,128)(2,1)} async-done(((bf16[16,2,64,2048]{3,2,1,0:T(8,128)(2,1)}), bf16[16,2,64,2048]{3,2,1,0:T(8,128)(2,1)}, u32[]{:S(2)}, u32[]{:S(2)}) %all-to-all-start.2) | async-done | bytes 8388640 | tf_op jit(solution)/shard_map/all_to_all | solution.py:201
  628.9 13.3 %gather_fusion.1 = bf16[1024,2048]{1,0:T(8,128)(2,1)} fusion(bf16[2048,2048]{1,0:T(8,128)(2,1)} %bitcast.29, s32[1024]{0:T(1024)S(1)} %broadcast_clamp_fusion), kind=kCustom, calls=%fused_computation.1 | custom fusion | bytes 8392704 | tf_op jit(solution)/shard_map/jit(_take)/gather | solution.py:203
  642.2 5.6 multiply_reduce_fusion
  (309 shorter events, 112.9 us)
Async XLA Ops:
  6.5 8.8 %copy-start.2 = (f32[4,2048]{1,0:T(4,128)S(1)}, f32[4,2048]{1,0:T(4,128)}, u32[]{:S(2)}) copy-start(f32[4,2048]{1,0:T(4,128)} %param.25) | copy-start | bytes 98308
  6.5 8.9 %copy-start.7 = (f32[4]{0:T(128)S(1)}, f32[4]{0:T(128)}, u32[]{:S(2)}) copy-start(f32[4]{0:T(128)} %param.26) | copy-start | bytes 52
  6.5 172.4 %all-gather.2.cloned.1.call-start = ((), (), s32[]{:S(2)}) async-start(), calls=%async_computation.3 | async-start | bytes 17825792 | tf_op jit(solution)/shard_map/all_gather | solution.py:157
  138.5 3.8 copy-start.1
  142.3 11.4 %copy-start.5 = (s32[128,8]{0,1:T(8,128)S(1)}, s32[128,8]{0,1:T(8,128)}, u32[]{:S(2)}) copy-start(s32[128,8]{0,1:T(8,128)} %param.32) | copy-start | bytes 12292
  142.3 11.7 %copy-start.3 = (f32[4096]{0:T(1024)S(1)}, f32[4096]{0:T(1024)}, u32[]{:S(2)}) copy-start(f32[4096]{0:T(1024)} %param.29) | copy-start | bytes 49156
  142.3 21.2 %copy-start.8 = (s32[32]{0:T(128)S(1)}, s32[32]{0:T(128)}, u32[]{:S(2)}) copy-start(s32[32]{0:T(128)} %param.34) | copy-start | bytes 388
  147.0 31.6 %all-to-all-start = ((bf16[16,128,256]{2,1,0:T(8,128)(2,1)}), bf16[16,128,256]{2,1,0:T(8,128)(2,1)S(1)}, u32[]{:S(2)}, u32[]{:S(2)}) async-start(bf16[16,128,256]{2,1,0:T(8,128)(2,1)} %bitcast.11), calls=%async_computation | async-start | bytes 2097152 | tf_op jit(solution)/shard_map/all_to_all | solution.py:152
  190.3 5.4 copy-start
  190.3 5.7 copy-start.4
  211.9 197.6 %slice-start = ((s8[6291456]{0:T(1024)(128)(4,1)}), s8[4194304]{0:T(1024)(128)(4,1)S(1)}, s32[]{:S(2)}) async-start(s8[6291456]{0:T(1024)(128)(4,1)} %bitcast.248), calls=%async_computation.4 | async-start | bytes 8388608
  398.9 10.6 %slice-start.1 = ((s8[6291456]{0:T(1024)(128)(4,1)}), s8[2097152]{0:T(1024)(128)(4,1)S(1)}, s32[]{:S(2)}) async-start(s8[6291456]{0:T(1024)(128)(4,1)} %bitcast.248), calls=%async_computation.5 | async-start | bytes 4194304
  440.8 5.8 copy-start.6
  440.8 188.1 %all-to-all-start.2 = ((bf16[16,2,64,2048]{3,2,1,0:T(8,128)(2,1)}), bf16[16,2,64,2048]{3,2,1,0:T(8,128)(2,1)}, u32[]{:S(2)}, u32[]{:S(2)}) async-start(bf16[16,2,64,2048]{3,2,1,0:T(8,128)(2,1)} %copy.99), calls=%async_computation.2 | async-start | bytes 16777216 | tf_op jit(solution)/shard_map/all_to_all | solution.py:201
Sparse Core Ops, SparseCore 0:
  9.5 125.3 all-gather.1
where the time goes:
time: 658 us; the launch traced here: 656 us
  waiting for transfers between devices  193 us (29%)
  blocking collectives  187 us (28%)
  matrix products  118 us (18%)
  local copies, waits for them, and re-layouts  79.6 us (12%)
  other arithmetic  51.1 us (8%)
  between operations  13.8 us (2%)
  starting transfers between devices  12.5 us (2%)
    all_to_all x1, blocking collectives, local(): lax.all_to_all(send_rows, 'mix', split_axis=0, concat_axis=0, tiled=True)  187 us
    all_to_all x1, waiting for transfers between devices, local(): lax.all_to_all(result, 'mix', split_axis=0, concat_axis=0, tiled=True)  182 us
    another operation x20, other arithmetic  20.1 us
    dynamic_slice x32, local copies, waits for them, and re-layouts, scan_heads(): _, outputs = lax.scan(advance, empty_state, inputs)  19.4 us
    dot_general x8, matrix products, one_head(): output = jnp.dot(kernel * scores, drive_block, precision=highest)  17.2 us
    dot_general x8, matrix products, one_head(): jnp.einsum('qn,rpn->rqp', readout_wide, head_init, precision=highest)  14.9 us
    dot_general x1, matrix products, local(): jnp.einsum('sekf,efd->sekd', inner_act, w_down, preferred_element_type=jn...  14.5 us
    dot_general x8, matrix products, one_head(): jnp.dot((drive_block * last_weight[:, None]).T, basis_wide, precision=hig...  13.8 us
  transfers between devices with their start and end apart: 3, of which 2 were waited for; matrix products, arithmetic and copies ran while one was open for 23% of the time, Pallas kernels for 0%

commit v1 on v0

--- a/solution.py
+++ b/solution.py
@@ -7,6 +7,18 @@
 HEAD_DIM = 64
 SPAN = 256
 epsilon = 1e-05
+
+
+def in_blocks(x, dim, devices):
+    shape = x.shape
+    pieces = x.reshape(*shape[:dim], devices, shape[dim] // devices, *shape[dim + 1 :])
+    return jnp.moveaxis(pieces, dim, 0)
+
+
+def in_order(parts, dim):
+    dims = list(parts.shape[1:])
+    dims[dim] *= parts.shape[0]
+    return jnp.moveaxis(parts, 0, dim).reshape(dims)
 
 
 def request_layout(lengths, tokens_total):
@@ -198,7 +210,15 @@
     result = jnp.einsum(
         "sekf,efd->sekd", inner_act, w_down, preferred_element_type=jnp.float32
     ).astype(jnp.bfloat16)
-    returned_rows = lax.all_to_all(result, "mix", split_axis=0, concat_axis=0, tiled=True)
+    length, here = (lax.axis_size("mix"), lax.axis_index("mix"))
+    pieces = in_blocks(result, 0, length)
+    out = pieces
+    for step in range(1, length):
+        target, source_2 = ((here + step) % length, (here - step) % length)
+        sent = lax.dynamic_index_in_dim(pieces, target, 0)
+        other = lax.ppermute(sent, "mix", [(i, (i + step) % length) for i in range(length)])
+        out = lax.dynamic_update_slice_in_dim(out, other, source_2, axis=0)
+    returned_rows = in_order(out, 0)
     back_flat = returned_rows.reshape(experts_total * cap_slots, model_width)
     picked = jnp.take(back_flat, buffer_index, axis=0).reshape(tok_rows, top_count, model_width)
     expert_sum = jnp.sum(route_weight[:, :, None] * picked.astype(jnp.float32), axis=1)

time: 658 us -> 688 us (1.046)
  blocking collectives: 187 us -> 0 us
  waiting for transfers between devices: 193 us -> 369 us
  local copies, waits for them, and re-layouts: 79.6 us -> 102 us
    all_to_all x1 -> x0, blocking collectives: 187 us -> none  [local(): lax.all_to_all(send_rows, 'mix', split_axis=0, concat_axis=0, tiled=True)]
    ppermute x0 -> x15, waiting for transfers between devices: none -> 176 us  [local(): lax.ppermute(sent, 'mix', [(i, (i + step) % length) for i in range(length)])]
    dynamic_update_slice x0 -> x16, local copies, waits for them, and re-layouts: none -> 23.7 us  [local(): out = lax.dynamic_update_slice_in_dim(out, other, source_2, axis=0)]
    convert_element_type x1 -> x0, local copies, waits for them, and re-layouts: 8.25 us -> none  [local(): result = jnp.einsum('sekf,efd->sekd', inner_act, w_down, preferred_elemen...]
    ppermute x0 -> x15, starting transfers between devices: none -> 6.9 us  [local(): lax.ppermute(sent, 'mix', [(i, (i + step) % length) for i in range(length)])]
  transfers between devices with their start and end apart: 3 -> 18, of which waited for: 2 -> 12; matrix products, arithmetic and copies ran while one was open for 23% -> 25% of each run, Pallas kernels for 0% -> 0%
where the time goes in v1:
time: 688 us; the launch traced here: 683 us
  waiting for transfers between devices  369 us (54%)
  matrix products  124 us (18%)
  local copies, waits for them, and re-layouts  102 us (15%)
  other arithmetic  53.9 us (8%)
  starting transfers between devices  18.3 us (3%)
  between operations  14.3 us (2%)
    all_to_all x1, waiting for transfers between devices, local(): lax.all_to_all(send_rows, 'mix', split_axis=0, concat_axis=0, tiled=True)  182 us
    ppermute x15, waiting for transfers between devices, local(): lax.ppermute(sent, 'mix', [(i, (i + step) % length) for i in range(length)])  176 us
    dynamic_update_slice x16, local copies, waits for them, and re-layouts, local(): out = lax.dynamic_update_slice_in_dim(out, other, source_2, axis=0)  23.7 us
    dynamic_slice x32, local copies, waits for them, and re-layouts, scan_heads(): _, outputs = lax.scan(advance, empty_state, inputs)  20.5 us
    another operation x20, other arithmetic  20.1 us
    dot_general x8, matrix products, one_head(): output = jnp.dot(kernel * scores, drive_block, precision=highest)  17.2 us
    dot_general x8, matrix products, one_head(): jnp.einsum('qn,rpn->rqp', readout_wide, head_init, precision=highest)  14.9 us
    dot_general x1, matrix products, local(): jnp.einsum('sekf,efd->sekd', inner_act, w_down, preferred_element_type=jn...  14.5 us
  transfers between devices with their start and end apart: 18, of which 12 were waited for; matrix products, arithmetic and copies ran while one was open for 25% of the time, Pallas kernels for 0%

profile of v1, /device:TPU:15, one launch (start us, length us, event | category | flops | bytes accessed | tf_op | source)
XLA Modules:
  0.0 682.7 jit_solution(8164375477084490839)
XLA Ops:
  15.5 124.0 %while.13 = (s32[]{:T(128)}, f32[4,64,128]{2,1,0:T(8,128)S(1)}, f32[8,4,256,64]{2,3,1,0:T(8,128)}, f32[8,4,256,64]{2,0,3,1:T(8,128)}, s32[8,256]{1,0:T(8,128)S(1...) while((s32[]{:T(128)}, f32[4,64,128]{2,1,0:T(8,128)S(1)}, ...), condition=%wide.region_8.9_spmd.clone, body=%wide.region_3.8_spmd.clone.sunk | while | flops 1231164672 | bytes 6562225 | solution.py:122
  61.6 2.4 constant_dynamic-slice_fusion.7
  108.2 2.3 constant_dynamic-slice_fusion.7
  139.5 2.9 copy.89
  147.9 6.5 all-to-all-start
  154.8 9.0 %reduce-window.26 = s32[32,8,128]{2,1,0:T(8,128)S(1)} reduce-window(s32[32,8,128]{2,1,0:T(8,128)S(1)} %fusion.69, s32[]{:T(128)} %constant.287.clone.1), window={size=1x1x128 pad=0_0x0_0x127_0}, to_apply=%region_12.13 | reduce-window | flops 4161536 | bytes 262148 | tf_op jit(solution)/shard_map/reduce-window.3
  164.4 4.3 scatter_custom_fusion
  168.9 10.4 %all-to-all-done = bf16[16,128,256]{2,1,0:T(8,128)(2,1)S(1)} async-done(((bf16[16,128,256]{2,1,0:T(8,128)(2,1)}), bf16[16,128,256]{2,1,0:T(8,128)(2,1)S(1)}, u32[]{:S(2)}, u32[]{:S(2)}) %all-to-all-start) | async-done | bytes 1048608 | tf_op jit(solution)/shard_map/all_to_all | solution.py:164
  179.7 11.4 %convert_bitcast_fusion = bf16[128,16,2048]{2,0,1:T(8,128)(2,1)} fusion(bf16[16,256,2048]{2,1,0:T(8,128)(2,1)} %bitcast.256, bf16[16,128,256]{2,1,0:T(8,128)(2,1)S(1)} %all-to-all-done, f32[16,256]{1,0:T(8,128)S(1)} %mul.163), kind=kOutput, calls=%fused_computation.65 | convolution fusion | flops 2153250816 | bytes 26230784 | tf_op jit(solution)/shard_map/tgc,gcd->tgd/dot_general | solution.py:170
  191.0 5.3 convert_reduce_fusion
  197.1 11.0 %gather_fusion = bf16[2048,2048]{1,0:T(8,128)(2,1)} fusion(bf16[128,2048]{1,0:T(8,128)(2,1)S(1)} %multiply_convert_fusion, s32[2048]{0:T(1024)S(1)} %maximum_clamp_fusion), kind=kCustom, calls=%fused_computation | custom fusion | bytes 16785408 | tf_op jit(solution)/shard_map/jit(_take)/gather | solution.py:202
  208.1 7.4 %select_select_fusion = bf16[16,2,64,2048]{3,2,1,0:T(8,128)(2,1)} fusion(bf16[16,2,64,2048]{3,2,1,0:T(8,128)(2,1)} %bitcast.257, pred[16,2,64]{2,1,0:T(4,128)(4,1)S(1)} %broadcast_in_dim.137, pred[16,2,64]{2,1,0:T(4,128)(4,1)S(1)} %broadcast_in_dim.135), kind=kLoop, calls=%fused_computation.64 | loop fusion | flops 8388608 | bytes 16781312 | tf_op jit(solution)/shard_map/jit(_where)/select_n | solution.py:200
  215.4 4.9 all-to-all-start.1
  220.5 182.1 %all-to-all-done.1 = bf16[16,2,64,2048]{3,2,1,0:T(8,128)(2,1)} async-done(((bf16[16,2,64,2048]{3,2,1,0:T(8,128)(2,1)}), bf16[16,2,64,2048]{3,2,1,0:T(8,128)(2,1)}, u32[]{:S(2)}, u32[]{:S(2)}) %all-to-all-start.1) | async-done | bytes 8388640 | tf_op jit(solution)/shard_map/all_to_all | solution.py:206
  402.6 12.7 %fusion.39 = f32[2,16,64,768]{3,2,1,0:T(8,128)} fusion(bf16[16,2,64,2048]{3,2,1,0:T(8,128)(2,1)} %all-to-all-done.1, bf16[2,2048,768]{2,1,0:T(8,128)(2,1)} %param.36), kind=kOutput, calls=%fused_computation.66 | convolution fusion | flops 6442450944 | bytes 20971520 | tf_op jit(solution)/shard_map/sekd,edf->sekf/dot_general | solution.py:208
  415.3 12.6 %fusion.41 = f32[2,16,64,768]{3,2,1,0:T(8,128)} fusion(bf16[16,2,64,2048]{3,2,1,0:T(8,128)(2,1)} %all-to-all-done.1, bf16[2,2048,768]{2,1,0:T(8,128)(2,1)} %param.35), kind=kOutput, calls=%fused_computation.68 | convolution fusion | flops 6442450944 | bytes 20971520 | tf_op jit(solution)/shard_map/sekd,edf->sekf/dot_general | solution.py:207
  427.9 14.5 %fusion.51 = bf16[2,16,64,2048]{3,2,1,0:T(8,128)(2,1)} fusion(bf16[2,768,2048]{2,1,0:T(8,128)(2,1)} %param.37, f32[2,16,64,768]{3,2,1,0:T(8,128)} %fusion.39, f32[2,16,64,768]{3,2,1,0:T(8,128)} %fusion.41), kind=kOutput, calls=%fused_computation.81 | convolution fusion | flops 6456082432 | bytes 27262976 | tf_op jit(solution)/shard_map/sekf,efd->sekd/dot_general | solution.py:210
  442.4 6.0 dynamic-slice_bitcast_fusion.1
  451.8 3.6 collective-permute-start.4
  455.4 6.1 collective-permute-done
  463.6 9.3 %collective-permute-done.1 = bf16[1,1,2,64,2048]{4,3,0,2,1:T(8,128)(2,1)} collective-permute-done((bf16[1,1,2,64,2048]{4,3,0,2,1:T(8,128)(2,1)}, bf16[1,1,2,64,2048]{4,3,0,2,1:T(8,128)(2,1)}, u32[]{:S(2)}, u32[]{:S(2)}) %collective-permute-start.1) | collective-permute-done | bytes 524320 | tf_op jit(solution)/shard_map/ppermute | solution.py:219
  474.7 9.2 %collective-permute-done.2 = bf16[1,1,2,64,2048]{4,3,0,2,1:T(8,128)(2,1)} collective-permute-done((bf16[1,1,2,64,2048]{4,3,0,2,1:T(8,128)(2,1)}, bf16[1,1,2,64,2048]{4,3,0,2,1:T(8,128)(2,1)}, u32[]{:S(2)}, u32[]{:S(2)}) %collective-permute-start.2) | collective-permute-done | bytes 524320 | tf_op jit(solution)/shard_map/ppermute | solution.py:219
  485.8 59.9 %collective-permute-done.3 = bf16[1,1,2,64,2048]{4,3,0,2,1:T(8,128)(2,1)S(1)} collective-permute-done((bf16[1,1,2,64,2048]{4,3,0,2,1:T(8,128)(2,1)}, bf16[1,1,2,64,2048]{4,3,0,2,1:T(8,128)(2,1)S(1)}, u32[]{:S(2)}, u32[]{:S(2)}) %collective-permute-start.3) | collective-permute-done | bytes 524320 | tf_op jit(solution)/shard_map/ppermute | solution.py:219
  546.5 27.2 %collective-permute-done.4 = bf16[1,1,2,64,2048]{4,3,0,2,1:T(8,128)(2,1)S(1)} collective-permute-done((bf16[1,1,2,64,2048]{4,3,0,2,1:T(8,128)(2,1)}, bf16[1,1,2,64,2048]{4,3,0,2,1:T(8,128)(2,1)S(1)}, u32[]{:S(2)}, u32[]{:S(2)}) %collective-permute-start.4) | collective-permute-done | bytes 524320 | tf_op jit(solution)/shard_map/ppermute | solution.py:219
  574.6 16.0 %collective-permute-done.5 = bf16[1,1,2,64,2048]{4,3,0,2,1:T(8,128)(2,1)S(1)} collective-permute-done((bf16[1,1,2,64,2048]{4,3,0,2,1:T(8,128)(2,1)}, bf16[1,1,2,64,2048]{4,3,0,2,1:T(8,128)(2,1)S(1)}, u32[]{:S(2)}, u32[]{:S(2)}) %collective-permute-start.5) | collective-permute-done | bytes 524320 | tf_op jit(solution)/shard_map/ppermute | solution.py:219
  591.5 16.0 %collective-permute-done.6 = bf16[1,1,2,64,2048]{4,3,0,2,1:T(8,128)(2,1)S(1)} collective-permute-done((bf16[1,1,2,64,2048]{4,3,0,2,1:T(8,128)(2,1)}, bf16[1,1,2,64,2048]{4,3,0,2,1:T(8,128)(2,1)S(1)}, u32[]{:S(2)}, u32[]{:S(2)}) %collective-permute-start.6) | collective-permute-done | bytes 524320 | tf_op jit(solution)/shard_map/ppermute | solution.py:219
  608.3 16.0 %collective-permute-done.7 = bf16[1,1,2,64,2048]{4,3,0,2,1:T(8,128)(2,1)S(1)} collective-permute-done((bf16[1,1,2,64,2048]{4,3,0,2,1:T(8,128)(2,1)}, bf16[1,1,2,64,2048]{4,3,0,2,1:T(8,128)(2,1)S(1)}, u32[]{:S(2)}, u32[]{:S(2)}) %collective-permute-start.7) | collective-permute-done | bytes 524320 | tf_op jit(solution)/shard_map/ppermute | solution.py:219
  628.7 6.0 collective-permute-done.12
  635.6 10.4 %collective-permute-done.13 = bf16[1,1,2,64,2048]{4,3,0,2,1:T(8,128)(2,1)S(1)} collective-permute-done((bf16[1,1,2,64,2048]{4,3,0,2,1:T(8,128)(2,1)S(1)}, bf16[1,1,2,64,2048]{4,3,0,2,1:T(8,128)(2,1)S(1)}, u32[]{:S(2)}, u32[]{:S(2)}) %collective-permute-start.13) | collective-permute-done | bytes 524320 | tf_op jit(solution)/shard_map/ppermute | solution.py:219
  647.7 8.3 %copy.99 = bf16[16,1,2,64,2048]{4,3,2,0,1:T(8,128)(2,1)} copy(bf16[16,1,2,64,2048]{4,3,0,2,1:T(8,128)(2,1)} %constant_dynamic-update-slice_fusion.14) | data formatting | bytes 16777216 | tf_op jit(solution)/shard_map/dynamic_update_slice | solution.py:220
  655.9 13.3 %gather_fusion.1 = bf16[1024,2048]{1,0:T(8,128)(2,1)} fusion(bf16[2048,2048]{1,0:T(8,128)(2,1)} %bitcast.254, s32[1024]{0:T(1024)S(1)} %broadcast_clamp_fusion), kind=kCustom, calls=%fused_computation.1 | custom fusion | bytes 8392704 | tf_op jit(solution)/shard_map/jit(_take)/gather | solution.py:223
  669.2 5.6 multiply_reduce_fusion
  (349 shorter events, 155.0 us)
Async XLA Ops:
  6.5 8.8 %copy-start.2 = (f32[4,2048]{1,0:T(4,128)S(1)}, f32[4,2048]{1,0:T(4,128)}, u32[]{:S(2)}) copy-start(f32[4,2048]{1,0:T(4,128)} %param.25) | copy-start | bytes 98308
  6.5 8.8 %copy-start.7 = (f32[4]{0:T(128)S(1)}, f32[4]{0:T(128)}, u32[]{:S(2)}) copy-start(f32[4]{0:T(128)} %param.26) | copy-start | bytes 52
  6.5 173.1 %all-gather.2.cloned.1.call-start = ((), (), s32[]{:S(2)}) async-start(), calls=%async_computation.2 | async-start | bytes 17825792 | tf_op jit(solution)/shard_map/all_gather | solution.py:169
  139.5 3.8 copy-start.1
  142.4 12.1 %copy-start.5 = (s32[128,8]{0,1:T(8,128)S(1)}, s32[128,8]{0,1:T(8,128)}, u32[]{:S(2)}) copy-start(s32[128,8]{0,1:T(8,128)} %param.32) | copy-start | bytes 12292
  142.4 12.4 %copy-start.3 = (f32[4096]{0:T(1024)S(1)}, f32[4096]{0:T(1024)}, u32[]{:S(2)}) copy-start(f32[4096]{0:T(1024)} %param.29) | copy-start | bytes 49156
  142.4 21.9 %copy-start.8 = (s32[32]{0:T(128)S(1)}, s32[32]{0:T(128)}, u32[]{:S(2)}) copy-start(s32[32]{0:T(128)} %param.34) | copy-start | bytes 388
  147.9 31.4 %all-to-all-start = ((bf16[16,128,256]{2,1,0:T(8,128)(2,1)}), bf16[16,128,256]{2,1,0:T(8,128)(2,1)S(1)}, u32[]{:S(2)}, u32[]{:S(2)}) async-start(bf16[16,128,256]{2,1,0:T(8,128)(2,1)} %bitcast.11), calls=%async_computation | async-start | bytes 2097152 | tf_op jit(solution)/shard_map/all_to_all | solution.py:164
  191.0 5.4 copy-start
  191.0 5.7 copy-start.4
  215.4 187.2 %all-to-all-start.1 = ((bf16[16,2,64,2048]{3,2,1,0:T(8,128)(2,1)}), bf16[16,2,64,2048]{3,2,1,0:T(8,128)(2,1)}, u32[]{:S(2)}, u32[]{:S(2)}) async-start(bf16[16,2,64,2048]{3,2,1,0:T(8,128)(2,1)} %select_select_fusion), calls=%async_computation.1 | async-start | bytes 16777216 | tf_op jit(solution)/shard_map/all_to_all | solution.py:206
  442.4 8.3 %copy-start.6 = (f32[128,8]{0,1:T(8,128)S(1)}, f32[128,8]{0,1:T(8,128)}, u32[]{:S(2)}) copy-start(f32[128,8]{0,1:T(8,128)} %param.33) | copy-start | bytes 12292
  448.4 13.0 %collective-permute-start = (bf16[1,1,2,64,2048]{4,3,0,2,1:T(8,128)(2,1)}, bf16[1,1,2,64,2048]{4,3,0,2,1:T(8,128)(2,1)}, u32[]{:S(2)}, u32[]{:S(2)}) collective-permute-start(bf16[1,1,2,64,2048]{4,3,0,2,1:T(8,128)(2,1)} %get-tuple-element.208), channel_id=1, source_target_pairs={{0,1},{1,2},{2,3},{3,4},{4,5},{5,6},{6,7},{7,8},{8,9},{9,10},{10,1... | collective-permute-start | bytes 1572872 | tf_op jit(solution)/shard_map/ppermute | solution.py:219
  450.2 22.6 %collective-permute-start.1 = (bf16[1,1,2,64,2048]{4,3,0,2,1:T(8,128)(2,1)}, bf16[1,1,2,64,2048]{4,3,0,2,1:T(8,128)(2,1)}, u32[]{:S(2)}, u32[]{:S(2)}) collective-permute-start(bf16[1,1,2,64,2048]{4,3,0,2,1:T(8,128)(2,1)} %get-tuple-element.207), channel_id=1, source_target_pairs={{0,2},{1,3},{2,4},{3,5},{4,6},{5,7},{6,8},{7,9},{8,10},{9,11},{10,... | collective-permute-start | bytes 1572872 | tf_op jit(solution)/shard_map/ppermute | solution.py:219
  450.3 33.6 %collective-permute-start.2 = (bf16[1,1,2,64,2048]{4,3,0,2,1:T(8,128)(2,1)}, bf16[1,1,2,64,2048]{4,3,0,2,1:T(8,128)(2,1)}, u32[]{:S(2)}, u32[]{:S(2)}) collective-permute-start(bf16[1,1,2,64,2048]{4,3,0,2,1:T(8,128)(2,1)} %get-tuple-element.206), channel_id=1, source_target_pairs={{0,3},{1,4},{2,5},{3,6},{4,7},{5,8},{6,9},{7,10},{8,11},{9,12},{10... | collective-permute-start | bytes 1572872 | tf_op jit(solution)/shard_map/ppermute | solution.py:219
  450.9 94.9 %collective-permute-start.3 = (bf16[1,1,2,64,2048]{4,3,0,2,1:T(8,128)(2,1)}, bf16[1,1,2,64,2048]{4,3,0,2,1:T(8,128)(2,1)S(1)}, u32[]{:S(2)}, u32[]{:S(2)}) collective-permute-start(bf16[1,1,2,64,2048]{4,3,0,2,1:T(8,128)(2,1)} %get-tuple-element.205), channel_id=1, source_target_pairs={{0,4},{1,5},{2,6},{3,7},{4,8},{5,9},{6,10},{7,11},{8,12},{9,13},{1... | collective-permute-start | bytes 1572872 | tf_op jit(solution)/shard_map/ppermute | solution.py:219
  451.8 122.0 %collective-permute-start.4 = (bf16[1,1,2,64,2048]{4,3,0,2,1:T(8,128)(2,1)}, bf16[1,1,2,64,2048]{4,3,0,2,1:T(8,128)(2,1)S(1)}, u32[]{:S(2)}, u32[]{:S(2)}) collective-permute-start(bf16[1,1,2,64,2048]{4,3,0,2,1:T(8,128)(2,1)} %get-tuple-element.204), channel_id=1, source_target_pairs={{0,5},{1,6},{2,7},{3,8},{4,9},{5,10},{6,11},{7,12},{8,13},{9,14},{... | collective-permute-start | bytes 1572872 | tf_op jit(solution)/shard_map/ppermute | solution.py:219
  461.4 129.2 %collective-permute-start.5 = (bf16[1,1,2,64,2048]{4,3,0,2,1:T(8,128)(2,1)}, bf16[1,1,2,64,2048]{4,3,0,2,1:T(8,128)(2,1)S(1)}, u32[]{:S(2)}, u32[]{:S(2)}) collective-permute-start(bf16[1,1,2,64,2048]{4,3,0,2,1:T(8,128)(2,1)} %get-tuple-element.203), channel_id=1, source_target_pairs={{0,6},{1,7},{2,8},{3,9},{4,10},{5,11},{6,12},{7,13},{8,14},{9,15},... | collective-permute-start | bytes 1572872 | tf_op jit(solution)/shard_map/ppermute | solution.py:219
  472.8 134.7 %collective-permute-start.6 = (bf16[1,1,2,64,2048]{4,3,0,2,1:T(8,128)(2,1)}, bf16[1,1,2,64,2048]{4,3,0,2,1:T(8,128)(2,1)S(1)}, u32[]{:S(2)}, u32[]{:S(2)}) collective-permute-start(bf16[1,1,2,64,2048]{4,3,0,2,1:T(8,128)(2,1)} %get-tuple-element.202), channel_id=1, source_target_pairs={{0,7},{1,8},{2,9},{3,10},{4,11},{5,12},{6,13},{7,14},{8,15},{9,0},... | collective-permute-start | bytes 1572872 | tf_op jit(solution)/shard_map/ppermute | solution.py:219
  483.9 140.4 %collective-permute-start.7 = (bf16[1,1,2,64,2048]{4,3,0,2,1:T(8,128)(2,1)}, bf16[1,1,2,64,2048]{4,3,0,2,1:T(8,128)(2,1)S(1)}, u32[]{:S(2)}, u32[]{:S(2)}) collective-permute-start(bf16[1,1,2,64,2048]{4,3,0,2,1:T(8,128)(2,1)} %get-tuple-element.201), channel_id=1, source_target_pairs={{0,8},{1,9},{2,10},{3,11},{4,12},{5,13},{6,14},{7,15},{8,0},{9,1},... | collective-permute-start | bytes 1572872 | tf_op jit(solution)/shard_map/ppermute | solution.py:219
  545.7 79.5 %collective-permute-start.8 = (bf16[1,1,2,64,2048]{4,3,0,2,1:T(8,128)(2,1)}, bf16[1,1,2,64,2048]{4,3,0,2,1:T(8,128)(2,1)S(1)}, u32[]{:S(2)}, u32[]{:S(2)}) collective-permute-start(bf16[1,1,2,64,2048]{4,3,0,2,1:T(8,128)(2,1)} %get-tuple-element.200), channel_id=1, source_target_pairs={{0,9},{1,10},{2,11},{3,12},{4,13},{5,14},{6,15},{7,0},{8,1},{9,2},... | collective-permute-start | bytes 1572872 | tf_op jit(solution)/shard_map/ppermute | solution.py:219
  573.8 52.2 %collective-permute-start.9 = (bf16[1,1,2,64,2048]{4,3,0,2,1:T(8,128)(2,1)}, bf16[1,1,2,64,2048]{4,3,0,2,1:T(8,128)(2,1)S(1)}, u32[]{:S(2)}, u32[]{:S(2)}) collective-permute-start(bf16[1,1,2,64,2048]{4,3,0,2,1:T(8,128)(2,1)} %get-tuple-element.199), channel_id=1, source_target_pairs={{0,10},{1,11},{2,12},{3,13},{4,14},{5,15},{6,0},{7,1},{8,2},{9,3},... | collective-permute-start | bytes 1572872 | tf_op jit(solution)/shard_map/ppermute | solution.py:219
  590.6 36.4 %collective-permute-start.10 = (bf16[1,1,2,64,2048]{4,3,0,2,1:T(8,128)(2,1)}, bf16[1,1,2,64,2048]{4,3,0,2,1:T(8,128)(2,1)S(1)}, u32[]{:S(2)}, u32[]{:S(2)}) collective-permute-start(bf16[1,1,2,64,2048]{4,3,0,2,1:T(8,128)(2,1)} %get-tuple-element.198), channel_id=1, source_target_pairs={{0,11},{1,12},{2,13},{3,14},{4,15},{5,0},{6,1},{7,2},{8,3},{9,4},{... | collective-permute-start | bytes 1572872 | tf_op jit(solution)/shard_map/ppermute | solution.py:219
  607.5 20.4 %collective-permute-start.11 = (bf16[1,1,2,64,2048]{4,3,0,2,1:T(8,128)(2,1)}, bf16[1,1,2,64,2048]{4,3,0,2,1:T(8,128)(2,1)S(1)}, u32[]{:S(2)}, u32[]{:S(2)}) collective-permute-start(bf16[1,1,2,64,2048]{4,3,0,2,1:T(8,128)(2,1)} %get-tuple-element.197), channel_id=1, source_target_pairs={{0,12},{1,13},{2,14},{3,15},{4,0},{5,1},{6,2},{7,3},{8,4},{9,5},{1... | collective-permute-start | bytes 1572872 | tf_op jit(solution)/shard_map/ppermute | solution.py:219
  624.4 10.4 %collective-permute-start.12 = (bf16[1,1,2,64,2048]{4,3,0,2,1:T(8,128)(2,1)S(1)}, bf16[1,1,2,64,2048]{4,3,0,2,1:T(8,128)(2,1)S(1)}, u32[]{:S(2)}, u32[]{:S(2)}) collective-permute-start(bf16[1,1,2,64,2048]{4,3,0,2,1:T(8,128)(2,1)S(1)} %get-tuple-element.196), channel_id=1, source_target_pairs={{0,13},{1,14},{2,15},{3,0},{4,1},{5,2},{6,3},{7,4},{8,5},{9,6},{10... | collective-permute-start | bytes 1572872 | tf_op jit(solution)/shard_map/ppermute | solution.py:219
  625.2 20.8 %collective-permute-start.13 = (bf16[1,1,2,64,2048]{4,3,0,2,1:T(8,128)(2,1)S(1)}, bf16[1,1,2,64,2048]{4,3,0,2,1:T(8,128)(2,1)S(1)}, u32[]{:S(2)}, u32[]{:S(2)}) collective-permute-start(bf16[1,1,2,64,2048]{4,3,0,2,1:T(8,128)(2,1)S(1)} %get-tuple-element.195), channel_id=1, source_target_pairs={{0,14},{1,15},{2,0},{3,1},{4,2},{5,3},{6,4},{7,5},{8,6},{9,7},{10,... | collective-permute-start | bytes 1572872 | tf_op jit(solution)/shard_map/ppermute | solution.py:219
  626.0 20.8 %collective-permute-start.14 = (bf16[1,1,2,64,2048]{4,3,0,2,1:T(8,128)(2,1)S(1)}, bf16[1,1,2,64,2048]{4,3,0,2,1:T(8,128)(2,1)S(1)}, u32[]{:S(2)}, u32[]{:S(2)}) collective-permute-start(bf16[1,1,2,64,2048]{4,3,0,2,1:T(8,128)(2,1)S(1)} %get-tuple-element.194), channel_id=1, source_target_pairs={{0,15},{1,0},{2,1},{3,2},{4,3},{5,4},{6,5},{7,6},{8,7},{9,8},{10,9... | collective-permute-start | bytes 1572872 | tf_op jit(solution)/shard_map/ppermute | solution.py:219
Sparse Core Ops, SparseCore 0:
  9.5 125.3 all-gather.1
